TPU v7x, 32 devices: a whole 2x2x4 slice. The times are simulated.
32 devices in a mesh: hop: 4 (over z), node: 8 (over y, x, core).
Axes of the slice: x: 2, y: 2, z: 4, core: 2. Of those that a mesh axis runs over, the one named last changes fastest.
Arguments:
- child_features: bfloat16 [16384, 1024], P(('hop', 'node')), may hold values from -6 to 6
- child_type: int32 [16384], P(('hop', 'node')), may hold values 0 or 1
- parent_features: bfloat16 [16384, 1024], P(('hop', 'node')), may hold values from -6 to 6
- child_slot: int32 [32, 32, 32], P(('hop', 'node')), may hold values from 0 to 511
- parent_slot: int32 [32, 32, 32], P(('hop', 'node')), may hold values from 0 to 511
- importance: int32 [32, 32, 32], P(('hop', 'node')), may hold values from 0 to 16, as said below
- board_proj: bfloat16 [512, 1024], replicated, may hold values from -0.25 to 0.25
- board_bias: float32 [1024], replicated, may hold values from -3 to 3
- neigh_weight: bfloat16 [1024, 1024], replicated, may hold values from -0.1875 to 0.1875
- neigh_bias: float32 [1024], replicated, may hold values from -3 to 3
- comb_weight: bfloat16 [2048, 1024], replicated, may hold values from -0.125 to 0.125
- comb_bias: float32 [1024], replicated, may hold values from -3 to 3
- out_grad: bfloat16 [16384, 1024], P(('hop', 'node')), may hold values from -6 to 6
Outputs:
- embedding: bfloat16 [16384, 1024], P(('hop', 'node'))
- child_grad: bfloat16 [16384, 1024], P(('hop', 'node'))
- parent_grad: bfloat16 [16384, 1024], P(('hop', 'node'))
- board_proj_grad: float32 [512, 1024], replicated
- board_bias_grad: float32 [1024], replicated
- neigh_weight_grad: float32 [1024, 1024], replicated
- neigh_bias_grad: float32 [1024], replicated
- comb_weight_grad: float32 [2048, 1024], replicated
- comb_bias_grad: float32 [1024], replicated
Inputs may be any that keep to these rules, and one draw needn't show every extreme that they name: For receiver r and sender s, importance[r, s, k] is positive for k below a count c(r, s) and 0 from there on; c(r, s) <= 32, and in every draw one receiver has c = 32 from every sender.
All inputs are finite; a program needn't handle non-finite values. No bound on the sum of `child_type` on one device may be relied on, other than what follows from the above.
Results may differ from a plain program's by a relative error of at most 0.0069.
Values may be sent and summed in bfloat16 or wider, within the bound.
A program may use at most 128 MiB of HBM per device.

v0:
```python
import jax
import jax.numpy as jnp
from jax import lax
from jax.sharding import PartitionSpec as P

epsilon = 1e-06


def outer_sum(left, right):
    return lax.dot_general(
        left, right, (((0,), (0,)), ((), ())), preferred_element_type=jnp.float32
    )


def times_transposed(left, right):
    return lax.dot_general(
        left, right, (((1,), (1,)), ((), ())), preferred_element_type=jnp.float32
    )


def silu_slope(value):
    sigma = jax.nn.sigmoid(value)
    return sigma * (1.0 + value * (1.0 - sigma))


def send_rows(buffer):
    return lax.all_to_all(buffer, ("hop", "node"), split_axis=0, concat_axis=0, tiled=True)


def send_grads(buffer):
    return lax.all_to_all(buffer, ("hop", "node"), split_axis=0, concat_axis=0, tiled=True)


def sum_gradients(parts):
    return lax.psum((parts[0], parts[1], parts[2], parts[3], parts[4], parts[5]), ("hop", "node"))


def body(
    child_features,
    child_type,
    parent_features,
    child_slot,
    parent_slot,
    importance,
    board_proj,
    board_bias,
    neigh_weight,
    neigh_bias,
    comb_weight,
    comb_bias,
    out_grad,
):
    width_board = board_proj.shape[0]
    feat_width = child_features.shape[1]
    child_count = child_features.shape[0]
    parent_count = parent_features.shape[0]
    hidden_width = neigh_weight.shape[1]
    senders = child_slot.shape[1]
    capacity = child_slot.shape[2]
    board = (child_type == 1)[:, None]
    left_part = child_features[:, :width_board]
    board_pre = jnp.dot(left_part, board_proj, preferred_element_type=jnp.float32) + board_bias
    child_in = jnp.where(board, board_pre.astype(jnp.bfloat16), child_features)
    neigh_pre = jnp.dot(child_in, neigh_weight, preferred_element_type=jnp.float32) + neigh_bias
    neigh = jax.nn.silu(neigh_pre).astype(jnp.bfloat16)
    child_rows = child_slot.reshape(-1)
    outgoing = jnp.take(neigh, child_rows, axis=0).reshape(senders, capacity, hidden_width)
    incoming = send_rows(outgoing).reshape(senders * capacity, hidden_width)
    weights = importance.reshape(-1).astype(jnp.float32)
    targets = parent_slot.reshape(-1)
    matches = targets[None, :] == jnp.arange(parent_count, dtype=jnp.int32)[:, None]
    weighted = jnp.where(matches, weights[None, :], 0.0)
    total = jnp.maximum(jnp.sum(weighted, axis=1), 1.0)
    sums = jnp.dot(weighted.astype(jnp.bfloat16), incoming, preferred_element_type=jnp.float32)
    agg = sums / total[:, None]
    cat = jnp.concatenate([parent_features, agg.astype(jnp.bfloat16)], axis=1)
    comb_pre = jnp.dot(cat, comb_weight, preferred_element_type=jnp.float32) + comb_bias
    hidden_z = jax.nn.silu(comb_pre)
    inverse = lax.rsqrt(jnp.sum(hidden_z * hidden_z, axis=1, keepdims=True) + epsilon)
    normed = hidden_z * inverse
    embedding = normed.astype(jnp.bfloat16)
    grad_y = out_grad.astype(jnp.float32)
    grad_z = inverse * (grad_y - normed * jnp.sum(normed * grad_y, axis=1, keepdims=True))
    grad_comb = (grad_z * silu_slope(comb_pre)).astype(jnp.bfloat16)
    comb_weight_grad = outer_sum(cat, grad_comb)
    comb_bias_grad = jnp.sum(grad_comb.astype(jnp.float32), axis=0)
    grad_cat = times_transposed(grad_comb, comb_weight)
    parent_grad = grad_cat[:, :feat_width].astype(jnp.bfloat16)
    grad_scaled = grad_cat[:, feat_width:] / total[:, None]
    grad_edges = (jnp.take(grad_scaled, targets, axis=0) * weights[:, None]).astype(jnp.bfloat16)
    returned = send_grads(grad_edges.reshape(senders, capacity, hidden_width))
    grad_neigh = jax.ops.segment_sum(
        returned.reshape(senders * capacity, hidden_width).astype(jnp.float32),
        child_rows,
        num_segments=child_count,
    )
    grad_npre = (grad_neigh * silu_slope(neigh_pre)).astype(jnp.bfloat16)
    neigh_weight_grad = outer_sum(child_in, grad_npre)
    neigh_bias_grad = jnp.sum(grad_npre.astype(jnp.float32), axis=0)
    grad_in = times_transposed(grad_npre, neigh_weight)
    grad_board = jnp.where(board, grad_in, 0.0).astype(jnp.bfloat16)
    board_proj_grad = outer_sum(left_part, grad_board)
    board_bias_grad = jnp.sum(grad_board.astype(jnp.float32), axis=0)
    grad_left = times_transposed(grad_board, board_proj)
    padding = jnp.zeros((child_count, feat_width - width_board), jnp.float32)
    board_rows = jnp.concatenate([grad_left, padding], axis=1)
    child_grad = jnp.where(board, board_rows, grad_in).astype(jnp.bfloat16)
    summed = sum_gradients(
        (
            board_proj_grad,
            board_bias_grad,
            neigh_weight_grad,
            neigh_bias_grad,
            comb_weight_grad,
            comb_bias_grad,
        )
    )
    return (
        embedding,
        child_grad,
        parent_grad,
        summed[0],
        summed[1],
        summed[2],
        summed[3],
        summed[4],
        summed[5],
    )


def solution(mesh):
    in_specs = (
        P(("hop", "node"), None),
        P(("hop", "node")),
        P(("hop", "node"), None),
        P(("hop", "node"), None, None),
        P(("hop", "node"), None, None),
        P(("hop", "node"), None, None),
        P(),
        P(),
        P(),
        P(),
        P(),
        P(),
        P(("hop", "node"), None),
    )
    out_specs = (
        P(("hop", "node"), None),
        P(("hop", "node"), None),
        P(("hop", "node"), None),
        P(),
        P(),
        P(),
        P(),
        P(),
        P(),
    )
    return jax.shard_map(body, mesh=mesh, in_specs=in_specs, out_specs=out_specs, check_vma=False)
```

profile of v0, /device:TPU:0, one launch (start us, length us, event | category | flops | bytes accessed | tf_op | source)
XLA Modules:
  0.0 455.3 jit_solution(8756432768272491844)
XLA Ops:
  7.2 0.0 copy-start
  7.2 0.9 reshape.148
  8.1 0.7 compare_and_fusion.1
  8.9 0.7 broadcast_compare_fusion
  9.6 0.0 copy-start.12
  9.6 2.4 fusion.7
  12.0 0.0 copy-done
  12.0 0.0 copy-done.12
  12.0 0.0 copy-start.4
  12.1 2.7 multiply_convert_fusion.2
  14.8 0.0 copy-done.4
  14.8 5.3 %gather_fusion = bf16[1024,1024]{1,0:T(8,128)(2,1)} fusion(bf16[512,1024]{1,0:T(8,128)(2,1)S(1)} %get-tuple-element.33, s32[1024]{0:T(1024)S(1)} %broadcast_clamp_fusion.1), kind=kCustom, calls=%fused_computation | custom fusion | bytes 4198400 | tf_op jit(solution)/shard_map/jit(_take)/gather | solution.py:67
  20.1 3.2 broadcast_select_fusion
  23.3 0.0 copy-start.8
  23.3 0.0 copy-start.10
  23.3 7.4 %all-to-all-start = ((bf16[32,32,1024]{2,1,0:T(8,128)(2,1)}), bf16[32,32,1024]{2,1,0:T(8,128)(2,1)}, u32[]{:S(2)}, u32[]{:S(2)}) async-start(bf16[32,32,1024]{2,1,0:T(8,128)(2,1)} %broadcast_select_fusion), calls=%async_computation | async-start | bytes 4194304 | tf_op jit(solution)/shard_map/all_to_all | solution.py:27
  30.8 0.0 copy-done.8
  30.8 0.1 eq.23
  30.8 0.1 reshape.150
  30.9 0.0 copy-done.10
  30.9 0.1 convert_element_type.68
  31.0 0.3 select_reduce_fusion
  31.3 48.3 %all-to-all-done = bf16[32,32,1024]{2,1,0:T(8,128)(2,1)} async-done(((bf16[32,32,1024]{2,1,0:T(8,128)(2,1)}), bf16[32,32,1024]{2,1,0:T(8,128)(2,1)}, u32[]{:S(2)}, u32[]{:S(2)}) %all-to-all-start) | async-done | bytes 2097184 | tf_op jit(solution)/shard_map/all_to_all | solution.py:27
  79.6 0.0 copy-start.11
  79.6 3.0 divide_convert_fusion
  82.6 0.0 copy-done.11
  82.6 0.0 copy-done.13
  82.6 0.1 copy-done.14
  82.8 2.8 multiply_reduce_fusion
  85.5 0.0 copy-done.15
  85.5 0.0 copy-done.2
  85.5 0.8 fusion.2
  86.4 2.2 convert_reduce_fusion
  88.6 2.4 fusion.20
  91.0 0.0 copy-start.3
  91.0 1.9 copy-done.3
  92.9 1.6 slice_divide_fusion
  94.5 7.9 %gather_fusion.1 = f32[1024,1024]{1,0:T(8,128)} fusion(f32[512,1024]{1,0:T(8,128)} %slice_divide_fusion, s32[1024]{0:T(1024)S(1)} %broadcast_clamp_fusion), kind=kCustom, calls=%fused_computation.1 | custom fusion | bytes 8392704 | tf_op jit(solution)/shard_map/jit(_take)/gather | solution.py:90
  102.4 3.9 multiply_convert_fusion
  106.4 4.1 all-to-all-start.1
  110.5 0.0 all-reduce.5.cloned.1.call-start
  110.6 0.0 copy-done.9
  110.6 0.1 reshape.170
  110.6 7.3 %fusion.8 = f32[2048,1024]{1,0:T(8,128)} fusion(bf16[512,1024]{1,0:T(8,128)(2,1)S(1)} %get-tuple-element.25, bf16[512,1024]{1,0:T(8,128)(2,1)} %copy-done.15, bf16[512,1024]{1,0:T(8,128)(2,1)} %param.15), kind=kOutput, calls=%fused_computation.35 | convolution fusion | flops 2151677952 | bytes 11534336 | tf_op jit(solution)/shard_map/dot_general | solution.py:10
  118.0 41.4 %all-to-all-done.1 = bf16[32,32,1024]{2,1,0:T(8,128)(2,1)} async-done(((bf16[32,32,1024]{2,1,0:T(8,128)(2,1)}), bf16[32,32,1024]{2,1,0:T(8,128)(2,1)}, u32[]{:S(2)}, u32[]{:S(2)}) %all-to-all-start.1) | async-done | bytes 2097184 | tf_op jit(solution)/shard_map/all_to_all | solution.py:31
  159.4 11.1 %scatter_custom_fusion = f32[512,1024]{1,0:T(8,128)} fusion(s32[1024]{0:T(1024)S(1)} %reshape.170, bf16[1024,1024]{1,0:T(8,128)(2,1)} %bitcast.10, f32[]{:T(128)} %constant.21.clone.1), kind=kCustom, calls=%fused_computation.3 | custom fusion | flops 2097152 | bytes 4194308 | tf_op jit(solution)/shard_map/scatter-add | solution.py:92
  170.5 3.1 convert_reduce_fusion.1
  173.5 0.0 copy-start.5
  173.5 2.3 convert_reduce_fusion.2
  175.8 0.0 copy-done.5
  175.8 3.3 fusion.22
  179.1 0.0 copy-done.7
  179.1 2.1 convolution_bitcast_fusion
  181.2 0.0 all-reduce.5.cloned.1.call-update
  181.2 2.7 slice.25
  183.9 40.1 %all-reduce.1 = (f32[1024]{0:T(1024)}, f32[1024]{0:T(1024)}, f32[1024]{0:T(1024)}) all-reduce(f32[1024]{0:T(1024)S(1)} %get-tuple-element.28, f32[1024]{0:T(1024)S(1)} %get-tuple-element.26, f32[1024]{0:T(1024)S(1)} %get-tuple-element.24), channel_id=1, replica_groups=mesh['hop'=4,'node'=8] {'hop','node'}, use_global_device_ids=true, to_apply=%region_6.7 | all-reduce | flops 3072 | bytes 24576 | tf_op jit(solution)/shard_map/psum | solution.py:35
  224.0 2.1 fusion.21
  226.1 0.0 copy-done.6
  226.1 1.3 select_convert_fusion.1
  227.4 208.7 %all-reduce.5.cloned.1.call-done = (f32[512,1024]{0,1:T(8,128)}, f32[1024,1024]{1,0:T(8,128)}, f32[2048,1024]{1,0:T(8,128)}) async-done(((f32[512,1024]{0,1:T(8,128)}, f32[1024,1024]{1,0:T(8,128)}, f32[2048,1024]{1,0:T(8,128)}), (f32[512,1024]{0,1:T(8,128)}, f32[1024,1024]{1,0:T(8,128)}, f32[2048,1024]{1,0:T(8,128)})) %all-reduce.5.cloned.1.call-update) | async-done | bytes 14680080 | tf_op jit(solution)/shard_map/psum | solution.py:35
  436.1 2.9 copy.22
  439.0 5.1 %copy.26 = f32[1024,1024]{1,0:T(8,128)} copy(f32[1024,1024]{1,0:T(8,128)} %get-tuple-element.43) | data formatting | bytes 8388608
  444.0 1.1 copy-done.1
  445.1 3.4 copy.27
  (16 shorter events, 0.1 us)
Async XLA Ops:
  7.2 4.8 %copy-start = (bf16[1024,1024]{1,0:T(8,128)(2,1)S(1)}, bf16[1024,1024]{1,0:T(8,128)(2,1)}, u32[]{:S(2)}) copy-start(bf16[1024,1024]{1,0:T(8,128)(2,1)} %param.21) | copy-start | bytes 6291460
  9.6 2.5 copy-start.12
  12.0 2.8 copy-start.4
  23.3 7.4 %copy-start.8 = (s32[1,32,32]{2,1,0:T(8,128)S(1)}, s32[1,32,32]{2,1,0:T(8,128)}, u32[]{:S(2)}) copy-start(s32[1,32,32]{2,1,0:T(8,128)} %param.17) | copy-start | bytes 12292
  23.3 7.6 %copy-start.10 = (s32[1,32,32]{2,1,0:T(8,128)S(1)}, s32[1,32,32]{2,1,0:T(8,128)}, u32[]{:S(2)}) copy-start(s32[1,32,32]{2,1,0:T(8,128)} %param.18) | copy-start | bytes 12292
  23.3 56.3 %all-to-all-start = ((bf16[32,32,1024]{2,1,0:T(8,128)(2,1)}), bf16[32,32,1024]{2,1,0:T(8,128)(2,1)}, u32[]{:S(2)}, u32[]{:S(2)}) async-start(bf16[32,32,1024]{2,1,0:T(8,128)(2,1)} %broadcast_select_fusion), calls=%async_computation | async-start | bytes 4194304 | tf_op jit(solution)/shard_map/all_to_all | solution.py:27
  79.6 3.0 copy-start.11
  79.6 3.0 copy-start.13
  79.6 3.1 copy-start.14
  82.8 2.8 copy-start.15
  82.8 2.8 copy-start.2
  91.0 2.0 copy-start.3
  106.4 4.2 copy-start.9
  106.4 53.0 %all-to-all-start.1 = ((bf16[32,32,1024]{2,1,0:T(8,128)(2,1)}), bf16[32,32,1024]{2,1,0:T(8,128)(2,1)}, u32[]{:S(2)}, u32[]{:S(2)}) async-start(bf16[32,32,1024]{2,1,0:T(8,128)(2,1)} %multiply_convert_fusion), calls=%async_computation.1 | async-start | bytes 4194304 | tf_op jit(solution)/shard_map/all_to_all | solution.py:31
  110.5 325.6 %all-reduce.5.cloned.1.call-start = ((), (), s32[]{:S(2)}) async-start(), calls=%async_computation.2 | async-start | bytes 29360128 | tf_op jit(solution)/shard_map/psum | solution.py:35
  173.5 2.3 copy-start.5
  175.8 3.3 copy-start.7
  224.0 2.1 copy-start.6
  438.9 6.2 %copy-start.1 = (f32[2048,1024]{1,0:T(8,128)S(1)}, f32[2048,1024]{1,0:T(8,128)}, u32[]{:S(2)}) copy-start(f32[2048,1024]{1,0:T(8,128)} %get-tuple-element.45) | copy-start | bytes 25165828
Sparse Core Ops, SparseCore 0:
  181.3 254.6 all-reduce.4
where the time goes:
time: 456 us; the launch traced here: 455 us
  waiting for transfers between devices  298 us (65%)
  blocking collectives  40.1 us (9%)
  local copies, waits for them, and re-layouts  31.8 us (7%)
  matrix products  30.4 us (7%)
  other arithmetic  28.9 us (6%)
  between operations  14.3 us (3%)
  starting transfers between devices  11.6 us (3%)
    psum x1, waiting for transfers between devices, sum_gradients(): lax.psum((parts[0], parts[1], parts[2], parts[3], parts[4], parts[5]), ('...  209 us
    all_to_all x1, waiting for transfers between devices, send_rows(): lax.all_to_all(buffer, ('hop', 'node'), split_axis=0, concat_axis=0, tile...  48.3 us
    all_to_all x1, waiting for transfers between devices, send_grads(): lax.all_to_all(buffer, ('hop', 'node'), split_axis=0, concat_axis=0, tile...  41.4 us
    psum x1, blocking collectives, sum_gradients(): lax.psum((parts[0], parts[1], parts[2], parts[3], parts[4], parts[5]), ('...  40.1 us
    unnamed x35, local copies, waits for them, and re-layouts  14.6 us
    dot_general x3, matrix products, outer_sum(): lax.dot_general(left, right, (((0,), (0,)), ((), ())), preferred_element_...  12.7 us
    scatter-add x1, other arithmetic, body(): jax.ops.segment_sum(returned.reshape(senders * capacity, hidden_width).as...  11.1 us
  transfers between devices with their start and end apart: 3, of which 3 were waited for; matrix products, arithmetic and copies ran while one was open for 3% of the time, Pallas kernels for 0%

commit v1 on v0

--- a/solution.py
+++ b/solution.py
@@ -4,6 +4,11 @@
 from jax.sharding import PartitionSpec as P
 
 epsilon = 1e-06
+
+
+def axis_by_axis(x, one, other):
+    partial = lax.psum(x, one)
+    return lax.psum(partial, other)
 
 
 def outer_sum(left, right):
@@ -32,7 +37,7 @@
 
 
 def sum_gradients(parts):
-    return lax.psum((parts[0], parts[1], parts[2], parts[3], parts[4], parts[5]), ("hop", "node"))
+    return axis_by_axis((parts[0], parts[1], parts[2], parts[3], parts[4], parts[5]), "node", "hop")
 
 
 def body(

time: 456 us -> 896 us (1.96)
  waiting for transfers between devices: 298 us -> 734 us
    psum x1 -> x2, waiting for transfers between devices: 209 us -> 644 us  [the longest x1 448 us: axis_by_axis(): return lax.psum(partial, other)]
    psum x1 -> x2, blocking collectives: 40.1 us -> 44.4 us  [the longest x1 24.5 us: axis_by_axis(): partial = lax.psum(x, one)]
  transfers between devices with their start and end apart: 3 -> 4, of which waited for: 3 -> 4; matrix products, arithmetic and copies ran while one was open for 3% -> 2% of each run, Pallas kernels for 0% -> 0%
where the time goes in v1:
time: 896 us; the launch traced here: 895 us
  waiting for transfers between devices  734 us (82%)
  blocking collectives  44.4 us (5%)
  local copies, waits for them, and re-layouts  31.8 us (4%)
  matrix products  30.3 us (3%)
  other arithmetic  28.9 us (3%)
  between operations  14.3 us (2%)
  starting transfers between devices  11.6 us (1%)
    psum x1, waiting for transfers between devices, axis_by_axis(): return lax.psum(partial, other)  448 us
    psum x1, waiting for transfers between devices, axis_by_axis(): partial = lax.psum(x, one)  195 us
    all_to_all x1, waiting for transfers between devices, send_rows(): lax.all_to_all(buffer, ('hop', 'node'), split_axis=0, concat_axis=0, tile...  48.3 us
    all_to_all x1, waiting for transfers between devices, send_grads(): lax.all_to_all(buffer, ('hop', 'node'), split_axis=0, concat_axis=0, tile...  41.4 us
    psum x1, blocking collectives, axis_by_axis(): partial = lax.psum(x, one)  24.5 us
    psum x1, blocking collectives, axis_by_axis(): return lax.psum(partial, other)  19.9 us
  transfers between devices with their start and end apart: 4, of which 4 were waited for; matrix products, arithmetic and copies ran while one was open for 2% of the time, Pallas kernels for 0%

profile of v1, /device:TPU:0, one launch (start us, length us, event | category | flops | bytes accessed | tf_op | source)
XLA Modules:
  0.0 894.8 jit_solution(5540197482688980256)
XLA Ops:
  7.2 0.0 copy-start
  7.2 0.9 reshape.148
  8.1 0.7 compare_and_fusion.1
  8.9 0.7 broadcast_compare_fusion
  9.6 0.0 copy-start.12
  9.6 2.4 fusion.7
  12.0 0.0 copy-done
  12.0 0.0 copy-done.12
  12.0 0.0 copy-start.4
  12.1 2.7 multiply_convert_fusion.2
  14.8 0.0 copy-done.4
  14.8 5.3 gather_fusion
  20.1 3.2 broadcast_select_fusion
  23.3 7.4 all-to-all-start
  30.8 0.0 copy-done.8
  30.8 0.1 eq.23
  30.8 0.1 reshape.150
  30.9 0.0 copy-done.10
  30.9 0.1 convert_element_type.68
  31.0 0.3 select_reduce_fusion
  31.3 48.3 %all-to-all-done = bf16[32,32,1024]{2,1,0:T(8,128)(2,1)} async-done(((bf16[32,32,1024]{2,1,0:T(8,128)(2,1)}), bf16[32,32,1024]{2,1,0:T(8,128)(2,1)}, u32[]{:S(2)}, u32[]{:S(2)}) %all-to-all-start) | async-done | bytes 2097184 | tf_op jit(solution)/shard_map/all_to_all | solution.py:32
  79.6 3.0 divide_convert_fusion
  82.6 0.0 copy-done.11
  82.6 0.0 copy-done.13
  82.6 0.1 copy-done.14
  82.8 2.8 multiply_reduce_fusion
  85.5 0.0 copy-done.15
  85.5 0.0 copy-done.2
  85.5 0.8 fusion.2
  86.4 2.2 convert_reduce_fusion
  88.6 2.4 fusion.20
  91.0 0.0 copy-start.3
  91.0 1.9 copy-done.3
  92.9 1.6 slice_divide_fusion
  94.5 7.9 gather_fusion.1
  102.4 3.9 multiply_convert_fusion
  106.4 4.1 all-to-all-start.1
  110.5 0.0 all-reduce.8.cloned.1.call-start
  110.5 0.0 copy-done.9
  110.5 0.1 reshape.170
  110.6 7.3 fusion.8
  117.9 41.4 %all-to-all-done.1 = bf16[32,32,1024]{2,1,0:T(8,128)(2,1)} async-done(((bf16[32,32,1024]{2,1,0:T(8,128)(2,1)}), bf16[32,32,1024]{2,1,0:T(8,128)(2,1)}, u32[]{:S(2)}, u32[]{:S(2)}) %all-to-all-start.1) | async-done | bytes 2097184 | tf_op jit(solution)/shard_map/all_to_all | solution.py:36
  159.4 11.1 %scatter_custom_fusion = f32[512,1024]{1,0:T(8,128)} fusion(s32[1024]{0:T(1024)S(1)} %reshape.170, bf16[1024,1024]{1,0:T(8,128)(2,1)} %bitcast.10, f32[]{:T(128)} %constant.21.clone.1), kind=kCustom, calls=%fused_computation.3 | custom fusion | flops 2097152 | bytes 4194308 | tf_op jit(solution)/shard_map/scatter-add | solution.py:97
  170.4 3.1 convert_reduce_fusion.1
  173.5 0.0 copy-start.5
  173.5 2.3 convert_reduce_fusion.2
  175.8 0.0 copy-done.5
  175.8 3.3 fusion.22
  179.1 0.0 copy-done.7
  179.1 2.1 convolution_bitcast_fusion
  181.2 0.0 all-reduce.8.cloned.1.call-update
  181.2 0.0 all-reduce.10.cloned.1.call-start
  181.2 195.5 %all-reduce.8.cloned.1.call-done = (f32[512,1024]{0,1:T(8,128)}, f32[1024,1024]{1,0:T(8,128)}, f32[2048,1024]{1,0:T(8,128)}) async-done(((f32[512,1024]{0,1:T(8,128)}, f32[1024,1024]{1,0:T(8,128)}, f32[2048,1024]{1,0:T(8,128)}), (f32[512,1024]{0,1:T(8,128)}, f32[1024,1024]{1,0:T(8,128)}, f32[2048,1024]{1,0:T(8,128)})) %all-reduce.8.cloned.1.call-update) | async-done | bytes 14680080 | tf_op jit(solution)/shard_map/psum | solution.py:10
  376.7 0.0 all-reduce.10.cloned.1.call-update
  376.7 2.7 slice.25
  379.5 24.5 %all-reduce.1 = (f32[1024]{0:T(1024)S(1)}, f32[1024]{0:T(1024)S(1)}, f32[1024]{0:T(1024)S(1)}) all-reduce(f32[1024]{0:T(1024)S(1)} %get-tuple-element.34, f32[1024]{0:T(1024)S(1)} %get-tuple-element.32, f32[1024]{0:T(1024)S(1)} %get-tuple-element.30), channel_id=1, replica_groups=mesh['hop'=4,'node'=8] {'node'}, use_global_device_ids=true, to_apply=%region_7.8 | all-reduce | flops 3072 | bytes 24576 | tf_op jit(solution)/shard_map/psum | solution.py:10
  404.0 19.9 %all-reduce.3 = (f32[1024]{0:T(1024)}, f32[1024]{0:T(1024)}, f32[1024]{0:T(1024)}) all-reduce(f32[1024]{0:T(1024)S(1)} %get-tuple-element.18, f32[1024]{0:T(1024)S(1)} %get-tuple-element.19, f32[1024]{0:T(1024)S(1)} %get-tuple-element.20), channel_id=1, replica_groups=mesh['hop'=4,'node'=8] {'hop'}, use_global_device_ids=true, to_apply=%region_8.9 | all-reduce | flops 3072 | bytes 24576 | tf_op jit(solution)/shard_map/psum | solution.py:11
  423.8 2.1 fusion.21
  425.9 1.3 select_convert_fusion.1
  427.2 448.4 %all-reduce.10.cloned.1.call-done = (f32[512,1024]{0,1:T(8,128)}, f32[1024,1024]{1,0:T(8,128)}, f32[2048,1024]{1,0:T(8,128)}) async-done(((f32[512,1024]{0,1:T(8,128)}, f32[1024,1024]{1,0:T(8,128)}, f32[2048,1024]{1,0:T(8,128)}), (f32[512,1024]{0,1:T(8,128)}, f32[1024,1024]{1,0:T(8,128)}, f32[2048,1024]{1,0:T(8,128)})) %all-reduce.10.cloned.1.call-update) | async-done | bytes 14680080 | tf_op jit(solution)/shard_map/psum | solution.py:11
  875.5 2.9 copy.22
  878.4 5.1 copy.29
  883.5 1.1 copy-done.1
  884.6 3.4 copy.30
  (20 shorter events, 0.1 us)
Async XLA Ops:
  7.2 4.8 copy-start
  9.6 2.5 copy-start.12
  12.0 2.8 copy-start.4
  23.3 7.4 copy-start.8
  23.3 7.6 copy-start.10
  23.3 56.3 %all-to-all-start = ((bf16[32,32,1024]{2,1,0:T(8,128)(2,1)}), bf16[32,32,1024]{2,1,0:T(8,128)(2,1)}, u32[]{:S(2)}, u32[]{:S(2)}) async-start(bf16[32,32,1024]{2,1,0:T(8,128)(2,1)} %broadcast_select_fusion), calls=%async_computation | async-start | bytes 4194304 | tf_op jit(solution)/shard_map/all_to_all | solution.py:32
  79.6 3.0 copy-start.11
  79.6 3.0 copy-start.13
  79.6 3.1 copy-start.14
  82.8 2.8 copy-start.15
  82.8 2.8 copy-start.2
  91.0 1.9 copy-start.3
  106.4 4.2 copy-start.9
  106.4 53.0 %all-to-all-start.1 = ((bf16[32,32,1024]{2,1,0:T(8,128)(2,1)}), bf16[32,32,1024]{2,1,0:T(8,128)(2,1)}, u32[]{:S(2)}, u32[]{:S(2)}) async-start(bf16[32,32,1024]{2,1,0:T(8,128)(2,1)} %multiply_convert_fusion), calls=%async_computation.1 | async-start | bytes 4194304 | tf_op jit(solution)/shard_map/all_to_all | solution.py:36
  110.5 266.2 %all-reduce.8.cloned.1.call-start = ((), (), s32[]{:S(2)}) async-start(), calls=%async_computation.2 | async-start | bytes 29360128 | tf_op jit(solution)/shard_map/psum | solution.py:10
  173.5 2.3 copy-start.5
  175.8 3.3 copy-start.7
  181.2 694.3 %all-reduce.10.cloned.1.call-start = ((), (), s32[]{:S(2)}) async-start(), calls=%async_computation.3 | async-start | bytes 29360128 | tf_op jit(solution)/shard_map/psum | solution.py:11
  423.8 2.1 copy-start.6
  878.4 6.2 copy-start.1
Sparse Core Ops, SparseCore 0:
  181.3 195.3 all-reduce.7
  379.8 495.7 all-reduce.9
